TPU v7x, 32 devices: a whole 2x2x4 slice. The times are simulated.
32 devices in a mesh: dp: 2 (over x), ha: 4 (over z), wa: 4 (over y, core).
Axes of the slice: x: 2, y: 2, z: 4, core: 2. Of those that a mesh axis runs over, the one named last changes fastest.
Arguments:
- query_in: bfloat16 [2, 4, 4, 384, 512], P('dp', 'ha', 'wa'), may hold values from -30 to 30
- key_in: bfloat16 [2, 4, 4, 384, 512], P('dp', 'ha', 'wa'), may hold values from -6 to 6
- value_in: bfloat16 [2, 4, 4, 384, 512], P('dp', 'ha', 'wa'), may hold values from -6 to 6
- grad_out: bfloat16 [2, 4, 4, 384, 3072], P('dp', 'ha', 'wa'), may hold values from -1.5 to 1.5
- out_weight: bfloat16 [512, 3072], P('dp'), may hold values from -0.25 to 0.25
Outputs:
- outcome: bfloat16 [2, 4, 4, 384, 3072], P('dp', 'ha', 'wa')
- query_grad: float32 [2, 4, 4, 384, 512], P('dp', 'ha', 'wa')
- key_grad: float32 [2, 4, 4, 384, 512], P('dp', 'ha', 'wa')
- value_grad: float32 [2, 4, 4, 384, 512], P('dp', 'ha', 'wa')
- weight_grad: float32 [512, 3072], P('dp')
All inputs are finite; a program needn't handle non-finite values.
Results may differ from a plain program's by a relative error of at most 0.035.
Values may be sent and summed in bfloat16 or wider, within the bound.
No kernel may reach another device: no remote copies, remote signals or barrier semaphores. Data moves between devices by JAX's collectives and lax.ppermute only.
A program may use at most 192 MiB of HBM per device.

v0:
```python
import jax
import jax.numpy as jnp
from jax import lax
from jax.sharding import PartitionSpec as P

HEADS = 4
SCALE_POWER = -0.5


def shortened(array):
    return jax.tree.map(lambda a: a.astype(jnp.bfloat16) if a.dtype == jnp.float32 else a, array)


def shifted(value, axis, steps):
    count = lax.axis_size(axis)
    first, last = (max(0, -steps), min(count, count - steps))
    return lax.ppermute(value, axis, [(source, source + steps) for source in range(first, last)])


def with_halo(array, sides, width):
    for axis, dim in sides:
        peers, length = (lax.axis_size(axis), array.shape[dim])
        up = [(i, (i + 1) % peers) for i in range(peers - 1)]
        down = [(j, i) for i, j in up]
        last = lax.slice_in_dim(array, length - width, length, axis=dim)
        first = lax.slice_in_dim(array, 0, width, axis=dim)
        before = lax.ppermute(last, axis, up)
        after = lax.ppermute(first, axis, down)
        array = jnp.concatenate([before, array, after], axis=dim)
    return array


def product(pattern, first_op, second_op):
    return jnp.einsum(pattern, first_op, second_op, preferred_element_type=jnp.float32)


def stack_window(extended, tile_cols):
    window_parts = []
    for row_off in range(3):
        for col_off in range(3):
            window_parts.append(extended[row_off, col_off : col_off + tile_cols])
    stacked = jnp.stack(window_parts, axis=1)
    return stacked.reshape((tile_cols, 9 * stacked.shape[2]) + stacked.shape[3:])


def window_keep(row_ok, col_ok, tile_cols, tile_len):
    flag_list = []
    for row_off in range(3):
        for col_off in range(3):
            flag_list.append(
                jnp.logical_and(row_ok[row_off], col_ok[col_off : col_off + tile_cols])
            )
    stacked = jnp.stack(flag_list, axis=1)
    return jnp.repeat(stacked, tile_len, axis=1)


def spread_window(stacked, tile_cols, tile_len):
    window_parts = stacked.reshape((tile_cols, 3, 3, tile_len) + stacked.shape[2:])
    spread_rows = []
    for row_off in range(3):
        gathered = None
        for col_off in range(3):
            placed = jnp.pad(
                window_parts[:, row_off, col_off], ((col_off, 2 - col_off), (0, 0), (0, 0))
            )
            gathered = placed if gathered is None else gathered + placed
        spread_rows.append(gathered)
    return jnp.stack(spread_rows)


def widen_rim(edge_part, axis_pos, length, at_first):
    expanded = jnp.expand_dims(edge_part, axis_pos)
    pad_spec = [(0, 0)] * expanded.ndim
    pad_spec[axis_pos] = (0, length - 1) if at_first else (length - 1, 0)
    return jnp.pad(expanded, pad_spec)


def attend_row(query_row, key_ext, value_ext, visible, head_count):
    tile_cols, tile_len, feature_width = query_row.shape
    head_dim = feature_width // head_count
    score_scale = head_dim**SCALE_POWER
    query_heads = query_row.reshape(tile_cols, tile_len, head_count, head_dim)
    key_heads = stack_window(key_ext, tile_cols).reshape(
        tile_cols, 9 * tile_len, head_count, head_dim
    )
    value_heads = stack_window(value_ext, tile_cols).reshape(
        tile_cols, 9 * tile_len, head_count, head_dim
    )
    scores = product("jqhd,jkhd->jhqk", query_heads, key_heads) * score_scale
    scores = jnp.where(visible[:, None, None, :], scores, -1e30)
    row_max = jnp.max(scores, axis=-1, keepdims=True)
    log_norm = row_max + jnp.log(jnp.sum(jnp.exp(scores - row_max), axis=-1, keepdims=True))
    soft_probs = jnp.exp(scores - log_norm).astype(jnp.bfloat16)
    attended = product("jhqk,jkhd->jqhd", soft_probs, value_heads)
    attended = attended.reshape(tile_cols, tile_len, feature_width).astype(jnp.bfloat16)
    return (attended, soft_probs, log_norm[..., 0])


def query_back(query_row, key_ext, value_ext, attended, grad_attn, soft_probs, head_count):
    tile_cols, tile_len, feature_width = query_row.shape
    head_dim = feature_width // head_count
    score_scale = head_dim**SCALE_POWER
    attended_heads = attended.astype(jnp.float32).reshape(tile_cols, tile_len, head_count, head_dim)
    grad_heads = grad_attn.reshape(tile_cols, tile_len, head_count, head_dim)
    row_delta = jnp.sum(attended_heads * grad_heads.astype(jnp.float32), axis=-1)
    row_delta = jnp.transpose(row_delta, (0, 2, 1))
    value_heads = stack_window(value_ext, tile_cols).reshape(
        tile_cols, 9 * tile_len, head_count, head_dim
    )
    prob_grad = product("jqhd,jkhd->jhqk", grad_heads, value_heads)
    score_grad = (soft_probs.astype(jnp.float32) * (prob_grad - row_delta[..., None])).astype(
        jnp.bfloat16
    )
    key_heads = stack_window(key_ext, tile_cols).reshape(
        tile_cols, 9 * tile_len, head_count, head_dim
    )
    query_grad = product("jhqk,jkhd->jqhd", score_grad, key_heads) * score_scale
    query_grad = query_grad.reshape(tile_cols, tile_len, feature_width)
    query_heads = query_row.reshape(tile_cols, tile_len, head_count, head_dim)
    key_part = (product("jhqk,jqhd->jkhd", score_grad, query_heads) * score_scale).reshape(
        tile_cols, 9 * tile_len, feature_width
    )
    value_part = product("jhqk,jqhd->jkhd", soft_probs, grad_heads).reshape(
        tile_cols, 9 * tile_len, feature_width
    )
    return (
        query_grad,
        row_delta,
        spread_window(key_part, tile_cols, tile_len),
        spread_window(value_part, tile_cols, tile_len),
    )


def send_rows(edge_part, offset):
    return shifted(shortened(edge_part), "ha", offset).astype(edge_part.dtype)


def send_columns(edge_part, offset):
    return shifted(shortened(edge_part), "wa", offset).astype(edge_part.dtype)


def on_device(query_in, key_in, value_in, grad_out, out_weight):
    clip_count, tile_rows, tile_cols, tile_len, feature_width = query_in.shape
    model_width = grad_out.shape[-1]
    head_count = HEADS
    row_first = lax.axis_index("ha") * tile_rows
    col_first = lax.axis_index("wa") * tile_cols
    all_rows = tile_rows * lax.axis_size("ha")
    all_cols = tile_cols * lax.axis_size("wa")
    row_global = row_first - 1 + jnp.arange(tile_rows + 2, dtype=jnp.int32)
    row_flags = jnp.logical_and(row_global >= 0, row_global < all_rows)
    col_global = col_first - 1 + jnp.arange(tile_cols + 2, dtype=jnp.int32)
    col_ok = jnp.logical_and(col_global >= 0, col_global < all_cols)
    full_weight = lax.all_gather(out_weight, "dp", axis=0, tiled=True)
    flat_grad = grad_out.reshape(-1, model_width)
    grad_attn = lax.dot_general(
        flat_grad, full_weight, (((1,), (1,)), ((), ())), preferred_element_type=jnp.float32
    )
    grad_attn = grad_attn.astype(jnp.bfloat16).reshape(query_in.shape)
    extended = with_halo(jnp.stack([key_in, value_in]), (("ha", 2), ("wa", 3)), 1)
    key_ext_all = extended[0]
    value_ext_all = extended[1]
    row_total = clip_count * tile_rows
    flat_rows = jnp.arange(row_total, dtype=jnp.int32)
    query_rows = query_in.reshape(row_total, tile_cols, tile_len, feature_width)
    grad_rows = grad_attn.reshape(row_total, tile_cols, tile_len, feature_width)

    def row_window(extended_all):
        return extended_all[0]

    def row_keep():
        return window_keep(row_flags, col_ok, tile_cols, tile_len)

    def forward_row(inputs):
        query_row, flat_index = inputs
        return attend_row(
            query_row, row_window(key_ext_all), row_window(value_ext_all), row_keep(), head_count
        )

    attended, soft_probs, log_norm = lax.map(forward_row, (query_rows, flat_rows))
    flat_attn = attended.reshape(-1, feature_width)
    outcome = jnp.dot(flat_attn, full_weight, preferred_element_type=jnp.float32).astype(
        jnp.bfloat16
    )
    outcome = outcome.reshape(clip_count, tile_rows, tile_cols, tile_len, model_width)

    def query_side(inputs):
        query_row, grad_row, attended_row, probs_row, flat_index = inputs
        query_grad, row_delta, key_part, value_part = query_back(
            query_row,
            row_window(key_ext_all),
            row_window(value_ext_all),
            attended_row,
            grad_row,
            probs_row,
            head_count,
        )
        return (query_grad, jnp.stack([key_part, value_part]))

    query_grad, ext_parts = lax.map(
        query_side, (query_rows, grad_rows, attended, soft_probs, flat_rows)
    )
    ext_parts = ext_parts.reshape(
        clip_count, tile_rows, 2, 3, tile_cols + 2, tile_len, feature_width
    )
    padded_grad = None
    for row_off in range(3):
        placed = jnp.pad(
            ext_parts[:, :, :, row_off],
            ((0, 0), (row_off, 2 - row_off), (0, 0), (0, 0), (0, 0), (0, 0)),
        )
        padded_grad = placed if padded_grad is None else padded_grad + placed
    from_below = send_rows(padded_grad[:, 0], -1)
    from_above = send_rows(padded_grad[:, tile_rows + 1], 1)
    middle = padded_grad[:, 1 : tile_rows + 1]
    middle = (
        middle
        + widen_rim(from_below, 1, tile_rows, False)
        + widen_rim(from_above, 1, tile_rows, True)
    )
    from_right = send_columns(middle[:, :, :, 0], -1)
    from_left = send_columns(middle[:, :, :, tile_cols + 1], 1)
    core_part = middle[:, :, :, 1 : tile_cols + 1]
    core_part = (
        core_part
        + widen_rim(from_right, 3, tile_cols, False)
        + widen_rim(from_left, 3, tile_cols, True)
    )
    key_grad = core_part[:, :, 0]
    value_grad = core_part[:, :, 1]
    query_grad = query_grad.reshape(query_in.shape)
    row_share = feature_width // lax.axis_size("dp")
    local_term = lax.dot_general(
        flat_attn, flat_grad, (((0,), (0,)), ((), ())), preferred_element_type=jnp.float32
    )
    summed = lax.psum(local_term, ("dp", "ha", "wa"))
    weight_grad = lax.dynamic_slice_in_dim(summed, lax.axis_index("dp") * row_share, row_share, 0)
    return (outcome, query_grad, key_grad, value_grad, weight_grad)


def solution(mesh):
    return jax.shard_map(
        on_device,
        mesh=mesh,
        in_specs=(
            P("dp", "ha", "wa", None, None),
            P("dp", "ha", "wa", None, None),
            P("dp", "ha", "wa", None, None),
            P("dp", "ha", "wa", None, None),
            P("dp", None),
        ),
        out_specs=(
            P("dp", "ha", "wa", None, None),
            P("dp", "ha", "wa", None, None),
            P("dp", "ha", "wa", None, None),
            P("dp", "ha", "wa", None, None),
            P("dp", None),
        ),
        check_vma=False,
    )
```

profile of v0, /device:TPU:0, one launch (start us, length us, event | category | flops | bytes accessed | tf_op | source)
XLA Modules:
  0.0 480.3 jit_solution(6171080770053422806)
XLA Ops:
  16.1 15.6 %collective-permute-done.1 = bf16[2,1,1,1,384,512]{5,4,3,2,1,0:T(8,128)(2,1)S(1)} collective-permute-done((bf16[2,1,1,1,384,512]{5,4,3,2,1,0:T(8,128)(2,1)S(1)}, bf16[2,1,1,1,384,512]{5,4,3,2,1,0:T(8,128)(2,1)S(1)}, u32[]{:S(2)}, u32[]{:S(2)}) %collective-permute-start.1) | collective-permute-done | bytes 786464 | tf_op jit(solution)/shard_map/ppermute | solution.py:28
  71.5 7.2 %reshape.242 = bf16[3456,4,128]{2,1,0:T(4,128)(2,1)} reshape(bf16[1,9,384,512]{3,2,1,0:T(8,128)(2,1)} %pad_maximum_fusion.2) | data formatting | bytes 7077888 | tf_op jit(solution)/shard_map/reshape.31
  78.7 6.9 %copy.102 = bf16[3456,4,128]{0,2,1:T(8,128)(2,1)} copy(bf16[3456,4,128]{2,1,0:T(4,128)(2,1)} %reshape.242) | data formatting | bytes 7077888 | tf_op jit(solution)/shard_map/reshape.31
  85.6 7.5 %bitcast_reduce_fusion = (f32[4,384]{1,0:T(4,128)S(1)}, f32[4,3456,384]{2,1,0:T(8,128)S(1)}) fusion(pred[3456]{0:T(1024)(128)(4,1)S(1)} %broadcast_in_dim.69, bf16[3456,4,128]{0,2,1:T(8,128)(2,1)} %copy.102, bf16[384,4,128]{2,1,0:T(4,128)(2,1)S(1)} %copy-done.9), kind=kOutput, calls=%fused_computation.2 | convolution fusion | flops 1374878208 | bytes 25175424 | tf_op jit(solution)/shard_map/while/body/eval_jaxpr/jqhd,jkhd->jhqk/dot_general | solution.py:34
  98.8 7.5 %fusion.3 = bf16[4,384,3456]{1,2,0:T(8,128)(2,1)} fusion(f32[4,3456,384]{2,1,0:T(8,128)S(1)} %get-tuple-element.125, f32[4,384]{1,0:T(4,128)S(1)} %log_add_fusion, pred[3456]{0:T(1024)(128)(4,1)S(1)} %broadcast_in_dim.69), kind=kLoop, calls=%fused_computation.6 | loop fusion | flops 21233664 | bytes 31860096 | tf_op jit(solution)/shard_map/while/body/eval_jaxpr/convert_element_type | solution.py:93
  108.2 7.4 %reshape.241 = bf16[3456,4,128]{2,1,0:T(4,128)(2,1)} reshape(bf16[1,9,384,512]{3,2,1,0:T(8,128)(2,1)} %pad_maximum_fusion.1) | data formatting | bytes 7077888 | tf_op jit(solution)/shard_map/reshape.41
  115.6 10.2 %convolution_bitcast_fusion = f32[1,3456,4,128]{1,3,2,0:T(8,128)} fusion(bf16[384,4,128]{0,2,1:T(8,128)(2,1)S(1)} %bitcast.185, bf16[4,384,3456]{1,2,0:T(8,128)(2,1)} %fusion.3), kind=kOutput, calls=%fused_computation.15 | convolution fusion | flops 1358954496 | bytes 18087936 | tf_op jit(solution)/shard_map/while/body/eval_jaxpr/jhqk,jqhd->jkhd/dot_general | solution.py:34
  125.8 6.3 %multiply_reduce_fusion = (f32[384,4]{0,1:T(4,128)S(1)}, bf16[4,128,384]{2,1,0:T(8,128)(2,1)S(1)}) fusion(f32[1,384,4,128]{1,3,2,0:T(8,128)S(1)} %bitcast.195, bf16[4,384,3456]{1,2,0:T(8,128)(2,1)} %fusion.3, bf16[3456,4,128]{2,1,0:T(4,128)(2,1)S(1)} %copy-done.2), kind=kOutput, calls=%fused_computation.75 | convolution fusion | flops 1359739392 | bytes 15341568 | tf_op jit(solution)/shard_map/while/body/eval_jaxpr/jhqk,jkhd->jqhd/dot_general | solution.py:34
  132.1 12.1 %multiply_convert_fusion = bf16[4,384,3456]{1,2,0:T(8,128)(2,1)} fusion(bf16[4,384,3456]{1,2,0:T(8,128)(2,1)} %fusion.3, bf16[384,4,128]{0,2,1:T(8,128)(2,1)S(1)} %bitcast.186, f32[4,384]{1,0:T(4,128)S(1)} %bitcast.197, bf16[3456,4,128]{2,1,0:T(4,128)(2,1)} %reshape.241), kind=kOutput, calls=%fused_computation.7 | convolution fusion | flops 1380188160 | bytes 25171968 | tf_op jit(solution)/shard_map/while/body/eval_jaxpr/jqhd,jkhd->jhqk/dot_general | solution.py:34
  144.2 9.2 %copy.108 = f32[1,3456,4,128]{3,2,0,1:T(4,128)} copy(f32[1,3456,4,128]{1,3,2,0:T(8,128)} %convolution_bitcast_fusion) | data formatting | bytes 14155776 | tf_op jit(solution)/shard_map/while/body/eval_jaxpr/jhqk,jqhd->jkhd/transpose | solution.py:34
  153.4 8.4 %slice_bitcast_fusion.23 = (f32[1,384,512]{2,0,1:T(1,128)S(1)}, f32[1,384,512]{2,0,1:T(1,128)}, f32[1,384,512]{2,0,1:T(1,128)}, f32[1,384,512]{2,0,1:T(1,128)}, ...) fusion(f32[1,3,3,384,512]{4,0,3,2,1:T(1,128)} %bitcast.183), kind=kLoop, calls=%fused_computation.64 | loop fusion | bytes 14155776 | tf_op jit(solution)/shard_map/while/body/eval_jaxpr/squeeze | solution.py:64
  164.7 15.1 %copy.105 = f32[1,3456,4,128]{3,2,0,1:T(4,128)S(1)} copy(f32[1,3456,4,128]{3,1,2,0:T(8,128)S(1)} %multiply_bitcast_fusion) | data formatting | bytes 14155776 | tf_op jit(solution)/shard_map/while/body/eval_jaxpr/mul | solution.py:120
  193.5 9.7 %maximum_bitcast_fusion.2 = f32[1,3,3,384,512]{4,2,3,1,0:T(4,128)} fusion(f32[1,3,384,512]{3,1,2,0:T(4,128)} %add_bitcast_fusion, f32[1,3,384,512]{3,1,2,0:T(4,128)} %add_bitcast_fusion.1, f32[1,3,384,512]{3,1,2,0:T(4,128)} %add_bitcast_fusion.2), kind=kLoop, calls=%fused_computation.12 | loop fusion | flops 3538944 | bytes 14155776 | tf_op jit(solution)/shard_map/while/body/eval_jaxpr/stack | solution.py:198
  214.5 9.7 %maximum_bitcast_fusion.1 = f32[1,3,3,384,512]{4,2,3,1,0:T(4,128)} fusion(f32[1,3,384,512]{3,1,2,0:T(4,128)} %add_bitcast_fusion.3, f32[1,3,384,512]{3,1,2,0:T(4,128)} %add_bitcast_fusion.4, f32[1,3,384,512]{3,1,2,0:T(4,128)} %add_bitcast_fusion.5), kind=kLoop, calls=%fused_computation.11 | loop fusion | flops 3538944 | bytes 14155776 | tf_op jit(solution)/shard_map/while/body/eval_jaxpr/stack | solution.py:198
  224.2 10.5 %maximum_bitcast_fusion = f32[1,1,2,3,3,384,512]{6,4,5,3,2,1,0:T(4,128)S(1)} fusion(f32[1,3,3,384,512]{4,2,3,1,0:T(4,128)} %maximum_bitcast_fusion.2, f32[1,3,3,384,512]{4,2,3,1,0:T(4,128)} %maximum_bitcast_fusion.1), kind=kLoop, calls=%fused_computation.9 | loop fusion | flops 3538944 | bytes 28311552 | tf_op jit(solution)/shard_map/reshape | solution.py:203
  234.6 7.7 %slice_bitcast_fusion.2 = (f32[1,1,2,3,384,512]{5,3,4,2,1,0:T(4,128)}, f32[1,1,2,3,384,512]{5,3,4,2,1,0:T(4,128)}, f32[1,1,2,3,384,512]{5,3,4,2,1,0:T(4,128)}) fusion(f32[1,1,2,3,3,384,512]{6,4,5,3,2,1,0:T(4,128)S(1)} %maximum_bitcast_fusion), kind=kLoop, calls=%fused_computation.20 | loop fusion | bytes 28311552 | tf_op jit(solution)/shard_map/squeeze | solution.py:209
  242.3 18.2 %pad_add_fusion = (f32[1,3,2,3,384,512]{5,3,4,2,1,0:T(4,128)}, bf16[1,3,2,3,384,512]{5,3,4,2,1,0:T(4,128)(2,1)S(1)}) fusion(f32[1,1,2,3,384,512]{5,3,4,2,1,0:T(4,128)} %get-tuple-element.86, f32[1,1,2,3,384,512]{5,3,4,2,1,0:T(4,128)} %get-tuple-element.87, f32[1,1,2,3,384,512]{5,3,4,2,1,0:T(4,128)} %get-tuple-element.85), kind=kLoop, calls=%fused_computation.10 | loop fusion | flops 10616832 | bytes 35389440 | tf_op jit(solution)/shard_map/add | solution.py:212
  277.2 63.5 %collective-permute-done.5 = bf16[1,2,3,384,512]{4,3,2,1,0:T(8,128)(2,1)} collective-permute-done((bf16[1,2,3,384,512]{4,3,2,1,0:T(8,128)(2,1)}, bf16[1,2,3,384,512]{4,3,2,1,0:T(8,128)(2,1)}, u32[]{:S(2)}, u32[]{:S(2)}) %collective-permute-start.5) | collective-permute-done | bytes 2359328 | tf_op jit(solution)/shard_map/ppermute | solution.py:17
  340.7 12.7 %collective-permute-done.4 = bf16[1,2,3,384,512]{4,3,2,1,0:T(8,128)(2,1)} collective-permute-done((bf16[1,2,3,384,512]{4,3,2,1,0:T(8,128)(2,1)}, bf16[1,2,3,384,512]{4,3,2,1,0:T(8,128)(2,1)}, u32[]{:S(2)}, u32[]{:S(2)}) %collective-permute-start.4) | collective-permute-done | bytes 2359328 | tf_op jit(solution)/shard_map/ppermute | solution.py:17
  353.5 10.7 %fusion.24 = (bf16[1,1,2,3,384,512]{5,3,4,2,1,0:T(4,128)(2,1)S(1)}, f32[1,1,2,3,384,512]{5,3,4,2,1,0:T(4,128)}) fusion(bf16[1,2,3,384,512]{4,3,2,1,0:T(8,128)(2,1)} %collective-permute-done.5, bf16[1,2,3,384,512]{4,3,2,1,0:T(8,128)(2,1)} %collective-permute-done.4, f32[1,3,2,3,384,512]{5,3,4,2,1,0:T(4,128)} %get-tuple-element.83), kind=kLoop, calls=%fused_computation.84 | loop fusion | flops 5898240 | bytes 16515072 | tf_op jit(solution)/shard_map/convert.6
  367.6 6.8 %collective-permute-start.7 = (bf16[1,1,2,384,512]{4,0,3,2,1:T(2,128)(2,1)}, bf16[1,1,2,384,512]{4,0,3,2,1:T(2,128)(2,1)}, u32[]{:S(2)}, u32[]{:S(2)}) collective-permute-start(bf16[1,1,2,384,512]{4,0,3,2,1:T(2,128)(2,1)} %get-tuple-element.115), channel_id=1, source_target_pairs={{0,1},{1,2},{2,3},{4,5},{5,6},{6,7},{8,9},{9,10},{10,11},{12,13},{... | collective-permute-start | bytes 2359304 | tf_op jit(solution)/shard_map/ppermute | solution.py:17
  375.7 7.2 %convolution_multiply_fusion = f32[4,128,384]{2,1,0:T(8,128)} fusion(bf16[3456,4,128]{0,2,1:T(8,128)(2,1)S(1)} %copy-done.3, bf16[4,384,3456]{1,2,0:T(8,128)(2,1)} %multiply_convert_fusion), kind=kOutput, calls=%fused_computation.45 | convolution fusion | flops 1359151104 | bytes 14942208 | tf_op jit(solution)/shard_map/while/body/eval_jaxpr/jhqk,jkhd->jqhd/dot_general | solution.py:34
  389.9 7.0 %fusion.13 = f32[1,1,2,1,384,512]{5,3,4,2,1,0:T(1,128)S(1)} fusion(f32[1,1,2,3,384,512]{5,3,4,2,1,0:T(4,128)} %get-tuple-element.82, bf16[1,1,2,384,512]{4,0,3,2,1:T(2,128)(2,1)} %collective-permute-done.7, bf16[1,1,2,384,512]{4,0,3,2,1:T(2,128)(2,1)} %collective-permute-done.6), kind=kLoop, calls=%fused_computation.44 | loop fusion | flops 1572864 | bytes 4718592 | tf_op jit(solution)/shard_map/add | solution.py:225
  399.9 69.5 %all-reduce.23.cloned.1.call-done = f32[512,3072]{1,0:T(8,128)} async-done(((f32[512,3072]{1,0:T(8,128)}), f32[512,3072]{1,0:T(8,128)}) %all-reduce.23.cloned.1.call-update) | async-done | bytes 6291472 | tf_op jit(solution)/shard_map/psum | solution.py:236
  (106 shorter events, 108.1 us)
Async XLA Ops:
  7.2 50.0 %copy-start = (bf16[1,1,1,384,3072]{4,3,2,1,0:T(8,128)(2,1)S(1)}, bf16[1,1,1,384,3072]{4,3,2,1,0:T(8,128)(2,1)}, u32[]{:S(2)}) copy-start(bf16[1,1,1,384,3072]{4,3,2,1,0:T(8,128)(2,1)} %param.8) | copy-start | bytes 7077892
  7.2 50.0 %all-gather.2.cloned.1.call-start = ((), (), s32[]{:S(2)}) async-start(), calls=%async_computation | async-start | bytes 4718592 | tf_op jit(solution)/shard_map/all_gather | solution.py:154
  7.9 46.0 %copy-start.25 = (bf16[1,1,1,384,512]{4,3,2,1,0:T(8,128)(2,1)S(1)}, bf16[1,1,1,384,512]{4,3,2,1,0:T(8,128)(2,1)}, u32[]{:S(2)}) copy-start(bf16[1,1,1,384,512]{4,3,2,1,0:T(8,128)(2,1)} %param.5) | copy-start | bytes 1179652
  7.9 461.5 %all-reduce.23.cloned.1.call-start = ((), (), s32[]{:S(2)}) async-start(), calls=%async_computation.1 | async-start | bytes 12582912 | tf_op jit(solution)/shard_map/psum | solution.py:236
  9.2 22.5 %collective-permute-start.1 = (bf16[2,1,1,1,384,512]{5,4,3,2,1,0:T(8,128)(2,1)S(1)}, bf16[2,1,1,1,384,512]{5,4,3,2,1,0:T(8,128)(2,1)S(1)}, u32[]{:S(2)}, u32[]{:S(2)}) collective-permute-start(bf16[2,1,1,1,384,512]{5,4,3,2,1,0:T(8,128)(2,1)S(1)} %pad_maximum_fusion.4), channel_id=1, source_target_pairs={{4,0},{8,4},{12,8},{5,1},{9,5},{13,9},{6,2},{10,6},{14,10},{7,3},{... | collective-permute-start | bytes 2359304 | tf_op jit(solution)/shard_map/ppermute | solution.py:28
  10.5 22.4 %collective-permute-start = (bf16[2,1,1,1,384,512]{5,4,3,2,1,0:T(8,128)(2,1)S(1)}, bf16[2,1,1,1,384,512]{5,4,3,2,1,0:T(8,128)(2,1)S(1)}, u32[]{:S(2)}, u32[]{:S(2)}) collective-permute-start(bf16[2,1,1,1,384,512]{5,4,3,2,1,0:T(8,128)(2,1)S(1)} %pad_maximum_fusion.4), channel_id=1, source_target_pairs={{0,4},{4,8},{8,12},{1,5},{5,9},{9,13},{2,6},{6,10},{10,14},{3,7},{... | collective-permute-start | bytes 2359304 | tf_op jit(solution)/shard_map/ppermute | solution.py:27
  35.9 27.6 %collective-permute-start.3 = (bf16[2,1,3,1,384,512]{5,4,3,2,1,0:T(8,128)(2,1)}, bf16[2,1,3,1,384,512]{5,4,3,2,1,0:T(8,128)(2,1)}, u32[]{:S(2)}, u32[]{:S(2)}) collective-permute-start(bf16[2,1,3,1,384,512]{5,4,3,2,1,0:T(8,128)(2,1)} %pad_maximum_fusion.3), channel_id=1, source_target_pairs={{1,0},{2,1},{3,2},{5,4},{6,5},{7,6},{9,8},{10,9},{11,10},{13,12},{... | collective-permute-start | bytes 7077896 | tf_op jit(solution)/shard_map/ppermute | solution.py:28
  37.2 26.3 %collective-permute-start.2 = (bf16[2,1,3,1,384,512]{5,4,3,2,1,0:T(8,128)(2,1)}, bf16[2,1,3,1,384,512]{5,4,3,2,1,0:T(8,128)(2,1)}, u32[]{:S(2)}, u32[]{:S(2)}) collective-permute-start(bf16[2,1,3,1,384,512]{5,4,3,2,1,0:T(8,128)(2,1)} %pad_maximum_fusion.3), channel_id=1, source_target_pairs={{0,1},{1,2},{2,3},{4,5},{5,6},{6,7},{8,9},{9,10},{10,11},{12,13},{... | collective-permute-start | bytes 7077896 | tf_op jit(solution)/shard_map/ppermute | solution.py:27
  54.9 8.7 %copy-start.7 = (bf16[1,1,1,384,512]{4,3,2,1,0:T(8,128)(2,1)S(1)}, bf16[1,1,1,384,512]{4,3,2,1,0:T(8,128)(2,1)}, u32[]{:S(2)}) copy-start(bf16[1,1,1,384,512]{4,3,2,1,0:T(8,128)(2,1)} %param.7) | copy-start | bytes 1179652
  54.9 8.7 %copy-start.8 = (bf16[1,1,1,384,512]{4,3,2,1,0:T(8,128)(2,1)S(1)}, bf16[1,1,1,384,512]{4,3,2,1,0:T(8,128)(2,1)}, u32[]{:S(2)}) copy-start(bf16[1,1,1,384,512]{4,3,2,1,0:T(8,128)(2,1)} %param.6) | copy-start | bytes 1179652
  78.7 6.9 %copy-start.9 = (bf16[384,4,128]{2,1,0:T(4,128)(2,1)S(1)}, bf16[384,4,128]{2,1,0:T(4,128)(2,1)}, u32[]{:S(2)}) copy-start(bf16[384,4,128]{2,1,0:T(4,128)(2,1)} %reshape.243) | copy-start | bytes 1179652
  98.7 7.5 %copy-start.4 = (bf16[1,3,384,512]{3,2,1,0:T(8,128)(2,1)S(1)}, bf16[1,3,384,512]{3,2,1,0:T(8,128)(2,1)}, u32[]{:S(2)}) copy-start(bf16[1,3,384,512]{3,2,1,0:T(8,128)(2,1)} %get-tuple-element.108) | copy-start | bytes 3538948
  98.8 7.5 %copy-start.5 = (bf16[1,3,384,512]{3,2,1,0:T(8,128)(2,1)S(1)}, bf16[1,3,384,512]{3,2,1,0:T(8,128)(2,1)}, u32[]{:S(2)}) copy-start(bf16[1,3,384,512]{3,2,1,0:T(8,128)(2,1)} %get-tuple-element.112) | copy-start | bytes 3538948
  98.8 7.5 %copy-start.6 = (bf16[1,3,384,512]{3,2,1,0:T(8,128)(2,1)S(1)}, bf16[1,3,384,512]{3,2,1,0:T(8,128)(2,1)}, u32[]{:S(2)}) copy-start(bf16[1,3,384,512]{3,2,1,0:T(8,128)(2,1)} %get-tuple-element.113) | copy-start | bytes 3538948
  115.6 10.2 %copy-start.2 = (bf16[3456,4,128]{2,1,0:T(4,128)(2,1)S(1)}, bf16[3456,4,128]{2,1,0:T(4,128)(2,1)}, u32[]{:S(2)}) copy-start(bf16[3456,4,128]{2,1,0:T(4,128)(2,1)} %reshape.241) | copy-start | bytes 10616836
  115.6 10.2 %copy-start.10 = (f32[384,512]{0,1:T(8,128)S(1)}, f32[384,512]{0,1:T(8,128)}, u32[]{:S(2)}) copy-start(f32[384,512]{0,1:T(8,128)} %copy.100) | copy-start | bytes 2359300
  153.4 8.4 %copy-start.1 = (bf16[4,384,3456]{1,2,0:T(8,128)(2,1)S(1)}, bf16[4,384,3456]{1,2,0:T(8,128)(2,1)}, u32[]{:S(2)}) copy-start(bf16[4,384,3456]{1,2,0:T(8,128)(2,1)} %multiply_convert_fusion) | copy-start | bytes 31850500
  203.2 4.5 copy-start.17
  203.2 4.5 copy-start.18
  264.8 76.0 %collective-permute-start.5 = (bf16[1,2,3,384,512]{4,3,2,1,0:T(8,128)(2,1)}, bf16[1,2,3,384,512]{4,3,2,1,0:T(8,128)(2,1)}, u32[]{:S(2)}, u32[]{:S(2)}) collective-permute-start(bf16[1,2,3,384,512]{4,3,2,1,0:T(8,128)(2,1)} %copy.113), channel_id=1, source_target_pairs={{0,4},{4,8},{8,12},{1,5},{5,9},{9,13},{2,6},{6,10},{10,14},{3,7},{... | collective-permute-start | bytes 7077896 | tf_op jit(solution)/shard_map/ppermute | solution.py:17
  271.5 82.0 %collective-permute-start.4 = (bf16[1,2,3,384,512]{4,3,2,1,0:T(8,128)(2,1)}, bf16[1,2,3,384,512]{4,3,2,1,0:T(8,128)(2,1)}, u32[]{:S(2)}, u32[]{:S(2)}) collective-permute-start(bf16[1,2,3,384,512]{4,3,2,1,0:T(8,128)(2,1)} %copy.111), channel_id=1, source_target_pairs={{4,0},{8,4},{12,8},{5,1},{9,5},{13,9},{6,2},{10,6},{14,10},{7,3},{... | collective-permute-start | bytes 7077896 | tf_op jit(solution)/shard_map/ppermute | solution.py:17
  364.2 11.5 %copy-start.3 = (bf16[3456,4,128]{0,2,1:T(8,128)(2,1)S(1)}, bf16[3456,4,128]{0,2,1:T(8,128)(2,1)}, u32[]{:S(2)}) copy-start(bf16[3456,4,128]{0,2,1:T(8,128)(2,1)} %copy.102) | copy-start | bytes 10616836
  367.6 22.3 %collective-permute-start.7 = (bf16[1,1,2,384,512]{4,0,3,2,1:T(2,128)(2,1)}, bf16[1,1,2,384,512]{4,0,3,2,1:T(2,128)(2,1)}, u32[]{:S(2)}, u32[]{:S(2)}) collective-permute-start(bf16[1,1,2,384,512]{4,0,3,2,1:T(2,128)(2,1)} %get-tuple-element.115), channel_id=1, source_target_pairs={{0,1},{1,2},{2,3},{4,5},{5,6},{6,7},{8,9},{9,10},{10,11},{12,13},{... | collective-permute-start | bytes 2359304 | tf_op jit(solution)/shard_map/ppermute | solution.py:17
  374.4 15.5 %collective-permute-start.6 = (bf16[1,1,2,384,512]{4,0,3,2,1:T(2,128)(2,1)}, bf16[1,1,2,384,512]{4,0,3,2,1:T(2,128)(2,1)}, u32[]{:S(2)}, u32[]{:S(2)}) collective-permute-start(bf16[1,1,2,384,512]{4,0,3,2,1:T(2,128)(2,1)} %get-tuple-element.114), channel_id=1, source_target_pairs={{1,0},{2,1},{3,2},{5,4},{6,5},{7,6},{9,8},{10,9},{11,10},{13,12},{... | collective-permute-start | bytes 2359304 | tf_op jit(solution)/shard_map/ppermute | solution.py:17
  (12 other events, 39.3 us)
Sparse Core Ops, SparseCore 0:
  9.5 47.6 all-gather.1
  277.4 191.9 all-reduce.22
where the time goes:
time: 490 us; the launch traced here: 480 us
  waiting for transfers between devices  166 us (34%)
  other arithmetic  112 us (23%)
  local copies, waits for them, and re-layouts  91.6 us (19%)
  matrix products  58.7 us (12%)
  starting transfers between devices  26.9 us (5%)
  between operations  26 us (5%)
    ppermute x4, waiting for transfers between devices, shifted(): lax.ppermute(value, axis, [(source, source + steps) for source in range(f...  76.2 us
    psum x1, waiting for transfers between devices, on_device(): summed = lax.psum(local_term, ('dp', 'ha', 'wa'))  69.5 us
    dot_general x6, matrix products, product(): jnp.einsum(pattern, first_op, second_op, preferred_element_type=jnp.float32)  46.2 us
    another operation x5, local copies, waits for them, and re-layouts  23.5 us
    another operation x6, other arithmetic, spread_window(): return jnp.stack(spread_rows)  20.8 us
    another operation x2, other arithmetic, query_side(): return (query_grad, jnp.stack([key_part, value_part]))  19.3 us
    add x1, other arithmetic, on_device(): padded_grad = placed if padded_grad is None else padded_grad + placed  18.2 us
    ppermute x2, waiting for transfers between devices, with_halo(): after = lax.ppermute(first, axis, down)  15.6 us
  transfers between devices with their start and end apart: 10, of which 6 were waited for; matrix products, arithmetic and copies ran while one was open for 12% of the time, Pallas kernels for 0%

commit v1 on v0

--- a/solution.py
+++ b/solution.py
@@ -233,7 +233,7 @@
     local_term = lax.dot_general(
         flat_attn, flat_grad, (((0,), (0,)), ((), ())), preferred_element_type=jnp.float32
     )
-    summed = lax.psum(local_term, ("dp", "ha", "wa"))
+    summed = lax.psum(lax.psum(local_term, ("ha", "wa")), "dp")
     weight_grad = lax.dynamic_slice_in_dim(summed, lax.axis_index("dp") * row_share, row_share, 0)
     return (outcome, query_grad, key_grad, value_grad, weight_grad)
 

time: 490 us -> 522 us (1.065)
  waiting for transfers between devices: 166 us -> 186 us
  local copies, waits for them, and re-layouts: 91.6 us -> 106 us
  starting transfers between devices: 26.9 us -> 20.5 us
    psum x1 -> x2, waiting for transfers between devices: 69.5 us -> 113 us  [on_device(): summed = lax.psum(lax.psum(local_term, ('ha', 'wa')), 'dp')]
    ppermute x4, waiting for transfers between devices: 76.2 us -> 53.4 us  [shifted(): lax.ppermute(value, axis, [(source, source + steps) for source in range(f...]
    mul x1, local copies, waits for them, and re-layouts: 15.1 us -> 25.5 us  [query_back(): product('jhqk,jqhd->jkhd', score_grad, query_heads) * score_scale]
    ppermute x4, starting transfers between devices: 14.1 us -> 7.73 us  [shifted(): lax.ppermute(value, axis, [(source, source + steps) for source in range(f...]
  transfers between devices with their start and end apart: 10 -> 11, of which waited for: 6 -> 7; matrix products, arithmetic and copies ran while one was open for 12% -> 27% of each run, Pallas kernels for 0% -> 0%
where the time goes in v1:
time: 522 us; the launch traced here: 512 us
  waiting for transfers between devices  186 us (36%)
  other arithmetic  115 us (22%)
  local copies, waits for them, and re-layouts  106 us (20%)
  matrix products  58.6 us (11%)
  between operations  26 us (5%)
  starting transfers between devices  20.5 us (4%)
    psum x2, waiting for transfers between devices, on_device(): summed = lax.psum(lax.psum(local_term, ('ha', 'wa')), 'dp')  113 us
    ppermute x4, waiting for transfers between devices, shifted(): lax.ppermute(value, axis, [(source, source + steps) for source in range(f...  53.4 us
    dot_general x6, matrix products, product(): jnp.einsum(pattern, first_op, second_op, preferred_element_type=jnp.float32)  46.2 us
    mul x1, local copies, waits for them, and re-layouts, query_back(): product('jhqk,jqhd->jkhd', score_grad, query_heads) * score_scale  25.5 us
    another operation x5, local copies, waits for them, and re-layouts  23.6 us
    another operation x2, other arithmetic, query_side(): return (query_grad, jnp.stack([key_part, value_part]))  20.5 us
    add x1, other arithmetic, on_device(): padded_grad = placed if padded_grad is None else padded_grad + placed  19.3 us
    another operation x6, other arithmetic, spread_window(): return jnp.stack(spread_rows)  19 us
  transfers between devices with their start and end apart: 11, of which 7 were waited for; matrix products, arithmetic and copies ran while one was open for 27% of the time, Pallas kernels for 0%

profile of v1, /device:TPU:0, one launch (start us, length us, event | category | flops | bytes accessed | tf_op | source)
XLA Modules:
  0.0 512.2 jit_solution(5778976981825777403)
XLA Ops:
  16.1 15.6 %collective-permute-done.1 = bf16[2,1,1,1,384,512]{5,4,3,2,1,0:T(8,128)(2,1)S(1)} collective-permute-done((bf16[2,1,1,1,384,512]{5,4,3,2,1,0:T(8,128)(2,1)S(1)}, bf16[2,1,1,1,384,512]{5,4,3,2,1,0:T(8,128)(2,1)S(1)}, u32[]{:S(2)}, u32[]{:S(2)}) %collective-permute-start.1) | collective-permute-done | bytes 786464 | tf_op jit(solution)/shard_map/ppermute | solution.py:28
  71.4 7.2 %reshape.242 = bf16[3456,4,128]{2,1,0:T(4,128)(2,1)} reshape(bf16[1,9,384,512]{3,2,1,0:T(8,128)(2,1)} %pad_maximum_fusion.2) | data formatting | bytes 7077888 | tf_op jit(solution)/shard_map/reshape.31
  78.7 6.8 %copy.102 = bf16[3456,4,128]{0,2,1:T(8,128)(2,1)} copy(bf16[3456,4,128]{2,1,0:T(4,128)(2,1)} %reshape.242) | data formatting | bytes 7077888 | tf_op jit(solution)/shard_map/reshape.31
  85.5 7.5 %bitcast_reduce_fusion = (f32[4,384]{1,0:T(4,128)S(1)}, f32[4,3456,384]{2,1,0:T(8,128)S(1)}) fusion(pred[3456]{0:T(1024)(128)(4,1)S(1)} %broadcast_in_dim.69, bf16[3456,4,128]{0,2,1:T(8,128)(2,1)} %copy.102, bf16[384,4,128]{2,1,0:T(4,128)(2,1)S(1)} %copy-done.10), kind=kOutput, calls=%fused_computation.2 | convolution fusion | flops 1374878208 | bytes 25175424 | tf_op jit(solution)/shard_map/while/body/eval_jaxpr/jqhd,jkhd->jhqk/dot_general | solution.py:34
  98.7 7.4 %fusion.3 = bf16[4,384,3456]{1,2,0:T(8,128)(2,1)} fusion(f32[4,3456,384]{2,1,0:T(8,128)S(1)} %get-tuple-element.125, f32[4,384]{1,0:T(4,128)S(1)} %log_add_fusion, pred[3456]{0:T(1024)(128)(4,1)S(1)} %broadcast_in_dim.69), kind=kLoop, calls=%fused_computation.6 | loop fusion | flops 21233664 | bytes 31860096 | tf_op jit(solution)/shard_map/while/body/eval_jaxpr/convert_element_type | solution.py:93
  108.0 7.5 %reshape.241 = bf16[3456,4,128]{2,1,0:T(4,128)(2,1)} reshape(bf16[1,9,384,512]{3,2,1,0:T(8,128)(2,1)} %pad_maximum_fusion.1) | data formatting | bytes 7077888 | tf_op jit(solution)/shard_map/reshape.41
  115.5 10.3 %convolution_bitcast_fusion = f32[1,3456,4,128]{1,3,2,0:T(8,128)} fusion(bf16[384,4,128]{0,2,1:T(8,128)(2,1)S(1)} %bitcast.185, bf16[4,384,3456]{1,2,0:T(8,128)(2,1)} %fusion.3), kind=kOutput, calls=%fused_computation.15 | convolution fusion | flops 1358954496 | bytes 18087936 | tf_op jit(solution)/shard_map/while/body/eval_jaxpr/jhqk,jqhd->jkhd/dot_general | solution.py:34
  125.8 6.3 %multiply_reduce_fusion = (f32[384,4]{0,1:T(4,128)S(1)}, bf16[4,128,384]{2,1,0:T(8,128)(2,1)S(1)}) fusion(f32[1,384,4,128]{1,3,2,0:T(8,128)S(1)} %bitcast.195, bf16[4,384,3456]{1,2,0:T(8,128)(2,1)} %fusion.3, bf16[3456,4,128]{2,1,0:T(4,128)(2,1)S(1)} %copy-done.3), kind=kOutput, calls=%fused_computation.75 | convolution fusion | flops 1359739392 | bytes 15341568 | tf_op jit(solution)/shard_map/while/body/eval_jaxpr/jhqk,jkhd->jqhd/dot_general | solution.py:34
  132.1 12.1 %multiply_convert_fusion = bf16[4,384,3456]{1,2,0:T(8,128)(2,1)} fusion(bf16[4,384,3456]{1,2,0:T(8,128)(2,1)} %fusion.3, bf16[384,4,128]{0,2,1:T(8,128)(2,1)S(1)} %bitcast.186, f32[4,384]{1,0:T(4,128)S(1)} %bitcast.197, bf16[3456,4,128]{2,1,0:T(4,128)(2,1)} %reshape.241), kind=kOutput, calls=%fused_computation.7 | convolution fusion | flops 1380188160 | bytes 25171968 | tf_op jit(solution)/shard_map/while/body/eval_jaxpr/jqhd,jkhd->jhqk/dot_general | solution.py:34
  144.2 9.1 %copy.108 = f32[1,3456,4,128]{3,2,0,1:T(4,128)} copy(f32[1,3456,4,128]{1,3,2,0:T(8,128)} %convolution_bitcast_fusion) | data formatting | bytes 14155776 | tf_op jit(solution)/shard_map/while/body/eval_jaxpr/jhqk,jqhd->jkhd/transpose | solution.py:34
  153.3 8.3 %slice_bitcast_fusion.23 = (f32[1,384,512]{2,0,1:T(1,128)}, f32[1,384,512]{2,0,1:T(1,128)}, f32[1,384,512]{2,0,1:T(1,128)}, f32[1,384,512]{2,0,1:T(1,128)}, f32[...) fusion(f32[1,3,3,384,512]{4,0,3,2,1:T(1,128)} %bitcast.183), kind=kLoop, calls=%fused_computation.64 | loop fusion | bytes 14155776 | tf_op jit(solution)/shard_map/while/body/eval_jaxpr/squeeze | solution.py:64
  164.6 25.5 %copy.105 = f32[1,3456,4,128]{3,2,0,1:T(4,128)S(1)} copy(f32[1,3456,4,128]{3,1,2,0:T(8,128)S(1)} %multiply_bitcast_fusion) | data formatting | bytes 14155776 | tf_op jit(solution)/shard_map/while/body/eval_jaxpr/mul | solution.py:120
  210.0 10.6 %maximum_bitcast_fusion.2 = f32[1,3,3,384,512]{4,2,3,1,0:T(4,128)} fusion(f32[1,3,384,512]{3,1,2,0:T(4,128)} %add_bitcast_fusion, f32[1,3,384,512]{3,1,2,0:T(4,128)} %add_bitcast_fusion.1, f32[1,3,384,512]{3,1,2,0:T(4,128)} %add_bitcast_fusion.2), kind=kLoop, calls=%fused_computation.12 | loop fusion | flops 3538944 | bytes 14155776 | tf_op jit(solution)/shard_map/while/body/eval_jaxpr/stack | solution.py:198
  230.2 9.8 %maximum_bitcast_fusion.1 = f32[1,3,3,384,512]{4,2,3,1,0:T(4,128)} fusion(f32[1,3,384,512]{3,1,2,0:T(4,128)} %add_bitcast_fusion.3, f32[1,3,384,512]{3,1,2,0:T(4,128)} %add_bitcast_fusion.4, f32[1,3,384,512]{3,1,2,0:T(4,128)} %add_bitcast_fusion.5), kind=kLoop, calls=%fused_computation.11 | loop fusion | flops 3538944 | bytes 14155776 | tf_op jit(solution)/shard_map/while/body/eval_jaxpr/stack | solution.py:198
  240.0 10.6 %maximum_bitcast_fusion = f32[1,1,2,3,3,384,512]{6,4,5,3,2,1,0:T(4,128)S(1)} fusion(f32[1,3,3,384,512]{4,2,3,1,0:T(4,128)} %maximum_bitcast_fusion.2, f32[1,3,3,384,512]{4,2,3,1,0:T(4,128)} %maximum_bitcast_fusion.1), kind=kLoop, calls=%fused_computation.9 | loop fusion | flops 3538944 | bytes 28311552 | tf_op jit(solution)/shard_map/reshape | solution.py:203
  250.6 7.9 %slice_bitcast_fusion.2 = (f32[1,1,2,3,384,512]{5,3,4,2,1,0:T(4,128)}, f32[1,1,2,3,384,512]{5,3,4,2,1,0:T(4,128)}, f32[1,1,2,3,384,512]{5,3,4,2,1,0:T(4,128)}) fusion(f32[1,1,2,3,3,384,512]{6,4,5,3,2,1,0:T(4,128)S(1)} %maximum_bitcast_fusion), kind=kLoop, calls=%fused_computation.20 | loop fusion | bytes 28311552 | tf_op jit(solution)/shard_map/squeeze | solution.py:209
  258.5 19.3 %pad_add_fusion = (f32[1,3,2,3,384,512]{5,3,4,2,1,0:T(4,128)}, bf16[1,3,2,3,384,512]{5,3,4,2,1,0:T(4,128)(2,1)}) fusion(f32[1,1,2,3,384,512]{5,3,4,2,1,0:T(4,128)} %get-tuple-element.86, f32[1,1,2,3,384,512]{5,3,4,2,1,0:T(4,128)} %get-tuple-element.87, f32[1,1,2,3,384,512]{5,3,4,2,1,0:T(4,128)} %get-tuple-element.85), kind=kLoop, calls=%fused_computation.10 | loop fusion | flops 10616832 | bytes 35389440 | tf_op jit(solution)/shard_map/add | solution.py:212
  277.9 67.7 %all-reduce.24.cloned.1.call-done = f32[512,3072]{1,0:T(8,128)} async-done(((f32[512,3072]{1,0:T(8,128)}), f32[512,3072]{1,0:T(8,128)}) %all-reduce.24.cloned.1.call-update) | async-done | bytes 6291472 | tf_op jit(solution)/shard_map/psum | solution.py:236
  358.9 47.1 %collective-permute-done.5 = bf16[1,2,3,384,512]{4,3,2,1,0:T(8,128)(2,1)S(1)} collective-permute-done((bf16[1,2,3,384,512]{4,3,2,1,0:T(8,128)(2,1)}, bf16[1,2,3,384,512]{4,3,2,1,0:T(8,128)(2,1)S(1)}, u32[]{:S(2)}, u32[]{:S(2)}) %collective-permute-start.5) | collective-permute-done | bytes 2359328 | tf_op jit(solution)/shard_map/ppermute | solution.py:17
  406.1 6.2 %collective-permute-done.4 = bf16[1,2,3,384,512]{4,3,2,1,0:T(8,128)(2,1)} collective-permute-done((bf16[1,2,3,384,512]{4,3,2,1,0:T(8,128)(2,1)}, bf16[1,2,3,384,512]{4,3,2,1,0:T(8,128)(2,1)}, u32[]{:S(2)}, u32[]{:S(2)}) %collective-permute-start.4) | collective-permute-done | bytes 2359328 | tf_op jit(solution)/shard_map/ppermute | solution.py:17
  412.3 13.0 %fusion.24 = (bf16[1,1,2,3,384,512]{5,3,4,2,1,0:T(4,128)(2,1)S(1)}, f32[1,1,2,3,384,512]{5,3,4,2,1,0:T(4,128)}) fusion(bf16[1,2,3,384,512]{4,3,2,1,0:T(8,128)(2,1)S(1)} %collective-permute-done.5, bf16[1,2,3,384,512]{4,3,2,1,0:T(8,128)(2,1)} %collective-permute-done.4, f32[1,3,2,3,384,512]{5,3,4,2,1,0:T(4,128)} %get-tuple-element.83), kind=kLoop, calls=%fused_computation.84 | loop fusion | flops 5898240 | bytes 16515072 | tf_op jit(solution)/shard_map/convert.6
  431.6 7.1 %convolution_multiply_fusion = f32[4,128,384]{2,1,0:T(8,128)S(1)} fusion(bf16[3456,4,128]{0,2,1:T(8,128)(2,1)S(1)} %copy-done.4, bf16[4,384,3456]{1,2,0:T(8,128)(2,1)} %multiply_convert_fusion), kind=kOutput, calls=%fused_computation.45 | convolution fusion | flops 1359151104 | bytes 14942208 | tf_op jit(solution)/shard_map/while/body/eval_jaxpr/jhqk,jkhd->jqhd/dot_general | solution.py:34
  445.7 7.1 %fusion.13 = f32[1,1,2,1,384,512]{5,3,4,2,1,0:T(1,128)S(1)} fusion(f32[1,1,2,3,384,512]{5,3,4,2,1,0:T(4,128)} %get-tuple-element.82, bf16[1,1,2,384,512]{4,0,3,2,1:T(2,128)(2,1)} %copy-done.33, bf16[1,1,2,384,512]{4,0,3,2,1:T(2,128)(2,1)} %collective-permute-done.6), kind=kLoop, calls=%fused_computation.44 | loop fusion | flops 1572864 | bytes 4718592 | tf_op jit(solution)/shard_map/add | solution.py:225
  455.7 45.6 %all-reduce.26.cloned.1.call-done = f32[512,3072]{1,0:T(8,128)} async-done(((f32[512,3072]{1,0:T(8,128)}), f32[512,3072]{1,0:T(8,128)}) %all-reduce.26.cloned.1.call-update) | async-done | bytes 6291472 | tf_op jit(solution)/shard_map/psum | solution.py:236
  (127 shorter events, 110.6 us)
Async XLA Ops:
  7.2 50.0 %copy-start = (bf16[1,1,1,384,3072]{4,3,2,1,0:T(8,128)(2,1)S(1)}, bf16[1,1,1,384,3072]{4,3,2,1,0:T(8,128)(2,1)}, u32[]{:S(2)}) copy-start(bf16[1,1,1,384,3072]{4,3,2,1,0:T(8,128)(2,1)} %param.8) | copy-start | bytes 7077892
  7.2 50.0 %all-gather.2.cloned.1.call-start = ((), (), s32[]{:S(2)}) async-start(), calls=%async_computation | async-start | bytes 4718592 | tf_op jit(solution)/shard_map/all_gather | solution.py:154
  7.9 46.1 %copy-start.34 = (bf16[1,1,1,384,512]{4,3,2,1,0:T(8,128)(2,1)S(1)}, bf16[1,1,1,384,512]{4,3,2,1,0:T(8,128)(2,1)}, u32[]{:S(2)}) copy-start(bf16[1,1,1,384,512]{4,3,2,1,0:T(8,128)(2,1)} %param.5) | copy-start | bytes 1179652
  7.9 337.6 %all-reduce.24.cloned.1.call-start = ((), (), s32[]{:S(2)}) async-start(), calls=%async_computation.1 | async-start | bytes 12582912 | tf_op jit(solution)/shard_map/psum | solution.py:236
  9.2 22.5 %collective-permute-start.1 = (bf16[2,1,1,1,384,512]{5,4,3,2,1,0:T(8,128)(2,1)S(1)}, bf16[2,1,1,1,384,512]{5,4,3,2,1,0:T(8,128)(2,1)S(1)}, u32[]{:S(2)}, u32[]{:S(2)}) collective-permute-start(bf16[2,1,1,1,384,512]{5,4,3,2,1,0:T(8,128)(2,1)S(1)} %pad_maximum_fusion.4), channel_id=1, source_target_pairs={{4,0},{8,4},{12,8},{5,1},{9,5},{13,9},{6,2},{10,6},{14,10},{7,3},{... | collective-permute-start | bytes 2359304 | tf_op jit(solution)/shard_map/ppermute | solution.py:28
  10.5 22.4 %collective-permute-start = (bf16[2,1,1,1,384,512]{5,4,3,2,1,0:T(8,128)(2,1)S(1)}, bf16[2,1,1,1,384,512]{5,4,3,2,1,0:T(8,128)(2,1)S(1)}, u32[]{:S(2)}, u32[]{:S(2)}) collective-permute-start(bf16[2,1,1,1,384,512]{5,4,3,2,1,0:T(8,128)(2,1)S(1)} %pad_maximum_fusion.4), channel_id=1, source_target_pairs={{0,4},{4,8},{8,12},{1,5},{5,9},{9,13},{2,6},{6,10},{10,14},{3,7},{... | collective-permute-start | bytes 2359304 | tf_op jit(solution)/shard_map/ppermute | solution.py:27
  36.0 27.6 %collective-permute-start.3 = (bf16[2,1,3,1,384,512]{5,4,3,2,1,0:T(8,128)(2,1)}, bf16[2,1,3,1,384,512]{5,4,3,2,1,0:T(8,128)(2,1)}, u32[]{:S(2)}, u32[]{:S(2)}) collective-permute-start(bf16[2,1,3,1,384,512]{5,4,3,2,1,0:T(8,128)(2,1)} %pad_maximum_fusion.3), channel_id=1, source_target_pairs={{1,0},{2,1},{3,2},{5,4},{6,5},{7,6},{9,8},{10,9},{11,10},{13,12},{... | collective-permute-start | bytes 7077896 | tf_op jit(solution)/shard_map/ppermute | solution.py:28
  37.2 26.3 %collective-permute-start.2 = (bf16[2,1,3,1,384,512]{5,4,3,2,1,0:T(8,128)(2,1)}, bf16[2,1,3,1,384,512]{5,4,3,2,1,0:T(8,128)(2,1)}, u32[]{:S(2)}, u32[]{:S(2)}) collective-permute-start(bf16[2,1,3,1,384,512]{5,4,3,2,1,0:T(8,128)(2,1)} %pad_maximum_fusion.3), channel_id=1, source_target_pairs={{0,1},{1,2},{2,3},{4,5},{5,6},{6,7},{8,9},{9,10},{10,11},{12,13},{... | collective-permute-start | bytes 7077896 | tf_op jit(solution)/shard_map/ppermute | solution.py:27
  54.9 8.7 %copy-start.8 = (bf16[1,1,1,384,512]{4,3,2,1,0:T(8,128)(2,1)S(1)}, bf16[1,1,1,384,512]{4,3,2,1,0:T(8,128)(2,1)}, u32[]{:S(2)}) copy-start(bf16[1,1,1,384,512]{4,3,2,1,0:T(8,128)(2,1)} %param.7) | copy-start | bytes 1179652
  54.9 8.7 %copy-start.9 = (bf16[1,1,1,384,512]{4,3,2,1,0:T(8,128)(2,1)S(1)}, bf16[1,1,1,384,512]{4,3,2,1,0:T(8,128)(2,1)}, u32[]{:S(2)}) copy-start(bf16[1,1,1,384,512]{4,3,2,1,0:T(8,128)(2,1)} %param.6) | copy-start | bytes 1179652
  98.7 7.4 %copy-start.5 = (bf16[1,3,384,512]{3,2,1,0:T(8,128)(2,1)S(1)}, bf16[1,3,384,512]{3,2,1,0:T(8,128)(2,1)}, u32[]{:S(2)}) copy-start(bf16[1,3,384,512]{3,2,1,0:T(8,128)(2,1)} %get-tuple-element.108) | copy-start | bytes 3538948
  98.7 7.4 %copy-start.6 = (bf16[1,3,384,512]{3,2,1,0:T(8,128)(2,1)S(1)}, bf16[1,3,384,512]{3,2,1,0:T(8,128)(2,1)}, u32[]{:S(2)}) copy-start(bf16[1,3,384,512]{3,2,1,0:T(8,128)(2,1)} %get-tuple-element.112) | copy-start | bytes 3538948
  115.5 10.3 %copy-start.3 = (bf16[3456,4,128]{2,1,0:T(4,128)(2,1)S(1)}, bf16[3456,4,128]{2,1,0:T(4,128)(2,1)}, u32[]{:S(2)}) copy-start(bf16[3456,4,128]{2,1,0:T(4,128)(2,1)} %reshape.241) | copy-start | bytes 10616836
  115.5 10.3 %copy-start.11 = (f32[384,512]{0,1:T(8,128)S(1)}, f32[384,512]{0,1:T(8,128)}, u32[]{:S(2)}) copy-start(f32[384,512]{0,1:T(8,128)} %copy.100) | copy-start | bytes 2359300
  153.3 8.3 %copy-start.2 = (bf16[4,384,3456]{1,2,0:T(8,128)(2,1)S(1)}, bf16[4,384,3456]{1,2,0:T(8,128)(2,1)}, u32[]{:S(2)}) copy-start(bf16[4,384,3456]{1,2,0:T(8,128)(2,1)} %multiply_convert_fusion) | copy-start | bytes 31850500
  198.8 302.5 %all-reduce.26.cloned.1.call-start = ((), (), s32[]{:S(2)}) async-start(), calls=%async_computation.2 | async-start | bytes 12582912 | tf_op jit(solution)/shard_map/psum | solution.py:236
  210.0 10.6 %copy-start.23 = (f32[1,384,512]{2,0,1:T(1,128)S(1)}, f32[1,384,512]{2,0,1:T(1,128)}, u32[]{:S(2)}) copy-start(f32[1,384,512]{2,0,1:T(1,128)} %get-tuple-element.91) | copy-start | bytes 2359300
  210.0 10.6 %copy-start.24 = (f32[1,384,512]{2,0,1:T(1,128)S(1)}, f32[1,384,512]{2,0,1:T(1,128)}, u32[]{:S(2)}) copy-start(f32[1,384,512]{2,0,1:T(1,128)} %get-tuple-element.92) | copy-start | bytes 2359300
  210.0 10.6 %copy-start.25 = (f32[1,384,512]{2,0,1:T(1,128)S(1)}, f32[1,384,512]{2,0,1:T(1,128)}, u32[]{:S(2)}) copy-start(f32[1,384,512]{2,0,1:T(1,128)} %get-tuple-element.93) | copy-start | bytes 2359300
  352.1 54.0 %collective-permute-start.5 = (bf16[1,2,3,384,512]{4,3,2,1,0:T(8,128)(2,1)}, bf16[1,2,3,384,512]{4,3,2,1,0:T(8,128)(2,1)S(1)}, u32[]{:S(2)}, u32[]{:S(2)}) collective-permute-start(bf16[1,2,3,384,512]{4,3,2,1,0:T(8,128)(2,1)} %copy.113), channel_id=1, source_target_pairs={{0,4},{4,8},{8,12},{1,5},{5,9},{9,13},{2,6},{6,10},{10,14},{3,7},{... | collective-permute-start | bytes 7077896 | tf_op jit(solution)/shard_map/ppermute | solution.py:17
  357.6 54.7 %collective-permute-start.4 = (bf16[1,2,3,384,512]{4,3,2,1,0:T(8,128)(2,1)}, bf16[1,2,3,384,512]{4,3,2,1,0:T(8,128)(2,1)}, u32[]{:S(2)}, u32[]{:S(2)}) collective-permute-start(bf16[1,2,3,384,512]{4,3,2,1,0:T(8,128)(2,1)} %copy.111), channel_id=1, source_target_pairs={{4,0},{8,4},{12,8},{5,1},{9,5},{13,9},{6,2},{10,6},{14,10},{7,3},{... | collective-permute-start | bytes 7077896 | tf_op jit(solution)/shard_map/ppermute | solution.py:17
  428.7 15.9 %collective-permute-start.7 = (bf16[1,1,2,384,512]{4,0,3,2,1:T(2,128)(2,1)}, bf16[1,1,2,384,512]{4,0,3,2,1:T(2,128)(2,1)S(1)}, u32[]{:S(2)}, u32[]{:S(2)}) collective-permute-start(bf16[1,1,2,384,512]{4,0,3,2,1:T(2,128)(2,1)} %get-tuple-element.115), channel_id=1, source_target_pairs={{0,1},{1,2},{2,3},{4,5},{5,6},{6,7},{8,9},{9,10},{10,11},{12,13},{... | collective-permute-start | bytes 2359304 | tf_op jit(solution)/shard_map/ppermute | solution.py:17
  430.1 14.5 %collective-permute-start.6 = (bf16[1,1,2,384,512]{4,0,3,2,1:T(2,128)(2,1)}, bf16[1,1,2,384,512]{4,0,3,2,1:T(2,128)(2,1)}, u32[]{:S(2)}, u32[]{:S(2)}) collective-permute-start(bf16[1,1,2,384,512]{4,0,3,2,1:T(2,128)(2,1)} %get-tuple-element.114), channel_id=1, source_target_pairs={{1,0},{2,1},{3,2},{5,4},{6,5},{7,6},{9,8},{10,9},{11,10},{13,12},{... | collective-permute-start | bytes 2359304 | tf_op jit(solution)/shard_map/ppermute | solution.py:17
  454.8 50.4 %copy-start.1 = (bf16[1,1,1,384,3072]{4,3,2,1,0:T(8,128)(2,1)S(1)}, bf16[1,1,1,384,3072]{4,3,2,1,0:T(8,128)(2,1)}, u32[]{:S(2)}) copy-start(bf16[1,1,1,384,3072]{4,3,2,1,0:T(8,128)(2,1)} %param.8) | copy-start | bytes 7077892
  (22 other events, 73.8 us)
Sparse Core Ops, SparseCore 0:
  9.5 47.6 all-gather.1
  198.9 146.5 all-reduce.23
  348.0 153.2 all-reduce.25
